TPU v7x, 128 devices: a whole 4x4x4 slice. The times are simulated.
128 devices in a mesh: tile: 8 (over x, core), gz: 16 (over y, z).
Axes of the slice: x: 4, y: 4, z: 4, core: 2. Of those that a mesh axis runs over, the one named last changes fastest.
Arguments:
- planes: bfloat16 [64, 3, 1024, 1024], P('gz', None, 'tile'), may hold values from -8 to 8
- level_gain: float32 [4], replicated, may hold values from 3 to 12
Outputs:
- joined: bfloat16 [3, 1024, 1024], P(None, ('tile', 'gz'))
All inputs are finite; a program needn't handle non-finite values.
Results may differ from a plain program's by a relative error of at most 0.0068.
The roundings to bfloat16 on the way count: a program that leaves them out, or rounds other values in their place, can miss the bound.
Values may be sent and summed in bfloat16 or wider, within the bound.
A program may use at most 192 MiB of HBM per device.

v0:
```python
import jax
import jax.numpy as jnp
from jax import lax
from jax.sharding import PartitionSpec as P

LEVELS = 4


TAPS = (0.0625, 0.25, 0.375, 0.25, 0.0625)


def extended_2(cells, sides, width):
    for axis, dim in sides:
        count = lax.axis_size(axis)
        ends = count - 1
        head = lax.slice_in_dim(cells, 0, width, axis=dim)
        tail = lax.slice_in_dim(cells, cells.shape[dim] - width, cells.shape[dim], axis=dim)
        cells = jnp.concatenate(
            [
                lax.ppermute(tail, axis, [(i, (i + 1) % count) for i in range(ends)]),
                cells,
                lax.ppermute(head, axis, [((i + 1) % count, i) for i in range(ends)]),
            ],
            axis=dim,
        )
    return cells


def combined_all(value, axis, join):
    pieces = jax.tree.map(lambda part: lax.all_gather(part, axis), value)
    head = jax.tree.map(lambda part: part[0], pieces)
    tail = jax.tree.map(lambda part: part[1:], pieces)
    total, _ = lax.scan(lambda total, share: (join(total, share), None), head, tail)
    return total


def taps_rows(field, stride):
    count = field.shape[1] - 4 * stride
    result = jnp.zeros((field.shape[0], count, field.shape[2]), jnp.float32)
    for place, factor in enumerate(TAPS):
        result = result + factor * field[:, place * stride : place * stride + count]
    return result


def smooth_cols(field, stride):
    count = field.shape[2]
    padded = jnp.pad(field, ((0, 0), (0, 0), (2 * stride, 2 * stride)))
    result = jnp.zeros_like(field)
    for place, factor in enumerate(TAPS):
        result = result + factor * padded[:, :, place * stride : place * stride + count]
    return result


def combine_states(first, second):
    top = jnp.maximum(first[0], second[0])
    scale_one = jnp.exp(first[0] - top)
    scale_two = jnp.exp(second[0] - top)
    rest = tuple(
        (left * scale_one + right * scale_two for left, right in zip(first[1:], second[1:]))
    )
    return (top,) + rest


def per_device(planes, level_gain):
    rows = planes.shape[2]
    luminance = (
        0.299 * planes[:, 0].astype(jnp.float32)
        + 0.587 * planes[:, 1].astype(jnp.float32)
        + 0.114 * planes[:, 2].astype(jnp.float32)
    ).astype(jnp.bfloat16)
    reach = 2 * (2**LEVELS - 1)
    extended = extended_2(luminance, (("tile", 1),), reach)
    approx = extended.astype(jnp.float32)
    first_row = lax.axis_index("tile") * rows - reach
    image_rows = rows * lax.axis_size("tile")
    energy = jnp.zeros(approx.shape, jnp.float32)
    offset = 0
    for level in range(LEVELS):
        stride = 2**level
        smoother = smooth_cols(taps_rows(approx, stride), stride)
        offset = offset + 2 * stride
        global_row = first_row + offset + jnp.arange(smoother.shape[1], dtype=jnp.int32)
        inside = (global_row >= 0) & (global_row < image_rows)
        smoother = jnp.where(inside[None, :, None], smoother, 0.0)
        detail = approx[:, 2 * stride : -2 * stride] - smoother
        energy = energy[:, 2 * stride : -2 * stride] + level_gain[level] * detail * detail
        approx = smoother
    local_peak = jnp.max(energy, axis=0)
    weight = jnp.exp(energy - local_peak[None])
    total = jnp.sum(weight, axis=0)
    colours = tuple(
        (jnp.sum(weight * planes[:, channel].astype(jnp.float32), axis=0) for channel in range(3))
    )
    share = rows // lax.axis_size("gz")
    merged = combined_all((local_peak, total) + colours, "gz", combine_states)
    start = lax.axis_index("gz") * share
    band_total = lax.dynamic_slice_in_dim(merged[1], start, share, 0)
    band_colour = jnp.stack(
        [lax.dynamic_slice_in_dim(merged[channel + 2], start, share, 0) for channel in range(3)]
    )
    joined = (band_colour / band_total[None]).astype(jnp.bfloat16)
    return joined


def solution(mesh):
    return jax.shard_map(
        per_device,
        mesh=mesh,
        in_specs=(P("gz", None, "tile", None), P()),
        out_specs=P(None, ("tile", "gz"), None),
        check_vma=False,
    )
```

profile of v0, /device:TPU:1, one launch (start us, length us, event | category | flops | bytes accessed | tf_op | source)
XLA Modules:
  0.0 475.8 jit_solution(16612627631634913368)
XLA Ops:
  6.5 2.6 fusion.56
  9.3 4.5 collective-permute-start
  13.8 1.9 collective-permute-start.1
  15.8 0.7 fusion.74
  16.4 0.6 collective-permute-done
  17.1 4.4 collective-permute-done.1
  21.5 0.4 maximum_convert_fusion
  21.9 0.3 slice.267
  22.2 1.7 fusion.14
  23.9 3.4 fusion.10
  27.3 0.3 slice.268
  27.6 1.3 fusion.27
  28.9 3.2 fusion.23
  32.1 1.0 fusion.72
  33.1 2.8 fusion.36
  35.9 0.5 fusion.63
  36.4 7.3 %fusion.70 = (f32[128,1024]{1,0:T(8,128)}, f32[4,128,1024]{2,1,0:T(8,128)}) fusion(f32[4,128,1024]{2,1,0:T(8,128)S(1)} %fusion.63, pred[128]{0:T(512)(128)(4,1)S(1)} %compare_and_fusion, f32[]{:T(128)} %bitcast.11, f32[4,160,1024]{2,1,0:T(8,128)S(1)} %fusion.36, f32[]{:T(128)} %bitcast.10, f32[4,160,1024]{2,1,0:T(8,128)S(1)} %get-tuple-element.104, ...), kind=kLoop, calls=%fused_computation.130 | loop fusion | flops 13500416 | bytes 13107344 | tf_op jit(solution)/shard_map/reduce_max | solution.py:88
  43.7 0.2 all-gather.13.cloned.1.call-start
  43.9 4.3 fusion.59
  48.3 0.7 all-gather.17.cloned.1.call-update
  49.0 0.5 all-gather.15.cloned.1.call-update
  49.6 0.5 all-gather.19.cloned.1.call-update
  50.1 66.2 %all-gather.11.cloned.1.call-done = f32[2048,1024]{1,0:T(8,128)} async-done(((f32[128,1024]{1,0:T(8,128)}), f32[2048,1024]{1,0:T(8,128)}) %all-gather.11.cloned.1.call-update) | async-done | bytes 8388624 | tf_op jit(solution)/shard_map/all_gather | solution.py:30
  116.3 7.8 %slice.292 = f32[1920,1024]{1,0:T(8,128)} slice(f32[2048,1024]{1,0:T(8,128)} %all-gather.11.cloned.1.call-done), slice={[128:2048], [0:1024]} | slice | bytes 15728640 | tf_op jit(solution)/shard_map/slice | solution.py:32
  124.1 64.8 %all-gather.13.cloned.1.call-done = f32[2048,1024]{1,0:T(8,128)} async-done(((f32[128,1024]{1,0:T(8,128)}), f32[2048,1024]{1,0:T(8,128)}) %all-gather.13.cloned.1.call-update) | async-done | bytes 8388624 | tf_op jit(solution)/shard_map/all_gather | solution.py:30
  188.9 7.8 %slice.293 = f32[1920,1024]{1,0:T(8,128)} slice(f32[2048,1024]{1,0:T(8,128)} %all-gather.13.cloned.1.call-done), slice={[128:2048], [0:1024]} | slice | bytes 15728640 | tf_op jit(solution)/shard_map/slice | solution.py:32
  196.8 64.8 %all-gather.17.cloned.1.call-done = f32[2048,1024]{1,0:T(8,128)} async-done(((f32[128,1024]{1,0:T(8,128)}), f32[2048,1024]{1,0:T(8,128)}) %all-gather.17.cloned.1.call-update) | async-done | bytes 8388624 | tf_op jit(solution)/shard_map/all_gather | solution.py:30
  261.5 8.0 %slice.295 = f32[1920,1024]{1,0:T(8,128)} slice(f32[2048,1024]{1,0:T(8,128)} %all-gather.17.cloned.1.call-done), slice={[128:2048], [0:1024]} | slice | bytes 15728640 | tf_op jit(solution)/shard_map/slice | solution.py:32
  269.5 64.5 %all-gather.15.cloned.1.call-done = f32[2048,1024]{1,0:T(8,128)} async-done(((f32[128,1024]{1,0:T(8,128)}), f32[2048,1024]{1,0:T(8,128)}) %all-gather.15.cloned.1.call-update) | async-done | bytes 8388624 | tf_op jit(solution)/shard_map/all_gather | solution.py:30
  334.0 7.9 %slice.294 = f32[1920,1024]{1,0:T(8,128)} slice(f32[2048,1024]{1,0:T(8,128)} %all-gather.15.cloned.1.call-done), slice={[128:2048], [0:1024]} | slice | bytes 15728640 | tf_op jit(solution)/shard_map/slice | solution.py:32
  341.9 64.6 %all-gather.19.cloned.1.call-done = f32[2048,1024]{1,0:T(8,128)} async-done(((f32[128,1024]{1,0:T(8,128)}), f32[2048,1024]{1,0:T(8,128)}) %all-gather.19.cloned.1.call-update) | async-done | bytes 8388624 | tf_op jit(solution)/shard_map/all_gather | solution.py:30
  406.5 8.1 %slice.296 = f32[1920,1024]{1,0:T(8,128)} slice(f32[2048,1024]{1,0:T(8,128)} %all-gather.19.cloned.1.call-done), slice={[128:2048], [0:1024]} | slice | bytes 15728640 | tf_op jit(solution)/shard_map/slice | solution.py:32
  414.7 53.9 %while.18 = (s32[]{:T(128)}, f32[128,1024]{1,0:T(8,128)S(1)}, f32[128,1024]{1,0:T(8,128)S(1)}, f32[128,1024]{1,0:T(8,128)S(1)}, f32[128,1024]{1,0:T(8,128)S(1)},...) while((s32[]{:T(128)}, f32[128,1024]{1,0:T(8,128)S(1)}, ...), condition=%wide.region_6.7_spmd, body=%wide.region_5.6_spmd.sunk | while | flops 1966082 | bytes 9961605 | solution.py:33
  414.7 1.7 fusion.77
  416.4 1.9 fusion.78
  418.3 1.7 fusion.77
  420.0 1.9 fusion.78
  421.9 1.7 fusion.77
  423.5 1.9 fusion.78
  425.5 1.7 fusion.77
  427.1 1.9 fusion.78
  429.1 1.7 fusion.77
  430.7 1.9 fusion.78
  432.7 1.7 fusion.77
  434.3 1.9 fusion.78
  436.2 1.7 fusion.77
  437.9 1.9 fusion.78
  439.8 1.7 fusion.77
  441.5 1.9 fusion.78
  443.4 1.7 fusion.77
  445.1 1.9 fusion.78
  447.0 1.7 fusion.77
  448.7 1.9 fusion.78
  450.6 1.7 fusion.77
  452.3 1.9 fusion.78
  454.2 1.7 fusion.77
  455.9 1.9 fusion.78
  457.8 1.7 fusion.77
  459.5 1.9 fusion.78
  461.4 1.7 fusion.77
  463.1 1.9 fusion.78
  465.0 1.7 fusion.77
  466.7 1.9 fusion.78
  468.6 0.6 fusion.68
  (28 shorter events, 0.3 us)
Async XLA Ops:
  6.5 9.2 %copy-start.1 = (f32[4]{0:T(128)S(1)}, f32[4]{0:T(128)}, u32[]{:S(2)}) copy-start(f32[4]{0:T(128)} %param.5) | copy-start | bytes 52
  6.5 109.8 %all-gather.11.cloned.1.call-start = ((), (), s32[]{:S(2)}) async-start(), calls=%async_computation | async-start | bytes 8912896 | tf_op jit(solution)/shard_map/all_gather | solution.py:30
  9.3 7.8 %collective-permute-start = (bf16[4,30,1024]{2,1,0:T(8,128)(2,1)S(1)}, bf16[4,30,1024]{2,1,0:T(8,128)(2,1)S(1)}, u32[]{:S(2)}, u32[]{:S(2)}) collective-permute-start(bf16[4,30,1024]{2,1,0:T(8,128)(2,1)S(1)} %get-tuple-element.106), channel_id=1, source_target_pairs={{0,16},{16,32},{32,48},{48,64},{64,80},{80,96},{96,112},{1,17},{17... | collective-permute-start | bytes 737288 | tf_op jit(solution)/shard_map/ppermute | solution.py:20
  13.8 7.7 %collective-permute-start.1 = (bf16[4,30,1024]{2,1,0:T(8,128)(2,1)S(1)}, bf16[4,30,1024]{2,1,0:T(8,128)(2,1)S(1)}, u32[]{:S(2)}, u32[]{:S(2)}) collective-permute-start(bf16[4,30,1024]{2,1,0:T(8,128)(2,1)S(1)} %get-tuple-element.107), channel_id=1, source_target_pairs={{16,0},{32,16},{48,32},{64,48},{80,64},{96,80},{112,96},{17,1},{33... | collective-permute-start | bytes 737288 | tf_op jit(solution)/shard_map/ppermute | solution.py:22
  36.4 7.5 %copy-start = (bf16[4,3,128,1024]{3,2,1,0:T(8,128)(2,1)S(1)}, bf16[4,3,128,1024]{3,2,1,0:T(8,128)(2,1)}, u32[]{:S(2)}) copy-start(bf16[4,3,128,1024]{3,2,1,0:T(8,128)(2,1)} %param.4) | copy-start | bytes 9437188
  43.7 145.2 %all-gather.13.cloned.1.call-start = ((), (), s32[]{:S(2)}) async-start(), calls=%async_computation.1 | async-start | bytes 8912896 | tf_op jit(solution)/shard_map/all_gather | solution.py:30
  48.2 213.3 %all-gather.17.cloned.1.call-start = ((), (), s32[]{:S(2)}) async-start(), calls=%async_computation.3 | async-start | bytes 8912896 | tf_op jit(solution)/shard_map/all_gather | solution.py:30
  49.0 285.1 %all-gather.15.cloned.1.call-start = ((), (), s32[]{:S(2)}) async-start(), calls=%async_computation.2 | async-start | bytes 8912896 | tf_op jit(solution)/shard_map/all_gather | solution.py:30
  49.5 356.9 %all-gather.19.cloned.1.call-start = ((), (), s32[]{:S(2)}) async-start(), calls=%async_computation.4 | async-start | bytes 8912896 | tf_op jit(solution)/shard_map/all_gather | solution.py:30
  406.5 8.2 %slice-start = ((f32[2048,1024]{1,0:T(8,128)}), f32[128,1024]{1,0:T(8,128)S(1)}, s32[]{:S(2)}) async-start(f32[2048,1024]{1,0:T(8,128)} %all-gather.13.cloned.1.call-done), calls=%async_computation.5 | async-start | bytes 1048576 | tf_op jit(solution)/shard_map/slice | solution.py:31
  406.5 8.2 %slice-start.1 = ((f32[2048,1024]{1,0:T(8,128)}), f32[128,1024]{1,0:T(8,128)S(1)}, s32[]{:S(2)}) async-start(f32[2048,1024]{1,0:T(8,128)} %all-gather.17.cloned.1.call-done), calls=%async_computation.6 | async-start | bytes 1048576 | tf_op jit(solution)/shard_map/slice | solution.py:31
  406.5 8.2 %slice-start.2 = ((f32[2048,1024]{1,0:T(8,128)}), f32[128,1024]{1,0:T(8,128)S(1)}, s32[]{:S(2)}) async-start(f32[2048,1024]{1,0:T(8,128)} %all-gather.15.cloned.1.call-done), calls=%async_computation.7 | async-start | bytes 1048576 | tf_op jit(solution)/shard_map/slice | solution.py:31
  406.5 8.2 %slice-start.3 = ((f32[2048,1024]{1,0:T(8,128)}), f32[128,1024]{1,0:T(8,128)S(1)}, s32[]{:S(2)}) async-start(f32[2048,1024]{1,0:T(8,128)} %all-gather.19.cloned.1.call-done), calls=%async_computation.8 | async-start | bytes 1048576 | tf_op jit(solution)/shard_map/slice | solution.py:31
  406.5 8.2 %slice-start.4 = ((f32[2048,1024]{1,0:T(8,128)}), f32[128,1024]{1,0:T(8,128)S(1)}, s32[]{:S(2)}) async-start(f32[2048,1024]{1,0:T(8,128)} %all-gather.11.cloned.1.call-done), calls=%async_computation.9 | async-start | bytes 1048576 | tf_op jit(solution)/shard_map/slice | solution.py:31
Sparse Core Ops, SparseCore 0:
  43.8 72.4 all-gather.10
  118.4 70.4 all-gather.12
  191.1 70.4 all-gather.16
  263.5 70.4 all-gather.14
  336.0 70.4 all-gather.18
where the time goes:
time: 477 us; the launch traced here: 476 us
  waiting for transfers between devices  332 us (70%)
  other arithmetic  82.8 us (17%)
  local copies, waits for them, and re-layouts  41 us (9%)
  between operations  13.4 us (3%)
  starting transfers between devices  6.77 us (1%)
    all_gather x5, waiting for transfers between devices, combined_all(): pieces = jax.tree.map(lambda part: lax.all_gather(part, axis), value)  325 us
    add x30, other arithmetic, combine_states(): left * scale_one + right * scale_two  53.7 us
    slice x5, local copies, waits for them, and re-layouts, combined_all(): tail = jax.tree.map(lambda part: part[1:], pieces)  39.7 us
  transfers between devices with their start and end apart: 7, of which 7 were waited for; matrix products, arithmetic and copies ran while one was open for 8% of the time, Pallas kernels for 0%

commit v1 on v0

--- a/solution.py
+++ b/solution.py
@@ -1,12 +1,16 @@
 import jax
 import jax.numpy as jnp
 from jax import lax
+from jax.experimental import pallas as pl
+from jax.experimental.pallas import tpu as pltpu
 from jax.sharding import PartitionSpec as P
 
 LEVELS = 4
 
 
 TAPS = (0.0625, 0.25, 0.375, 0.25, 0.0625)
+SIDE = 4
+HALF = 512
 
 
 def extended_2(cells, sides, width):
@@ -26,14 +30,6 @@
     return cells
 
 
-def combined_all(value, axis, join):
-    pieces = jax.tree.map(lambda part: lax.all_gather(part, axis), value)
-    head = jax.tree.map(lambda part: part[0], pieces)
-    tail = jax.tree.map(lambda part: part[1:], pieces)
-    total, _ = lax.scan(lambda total, share: (join(total, share), None), head, tail)
-    return total
-
-
 def taps_rows(field, stride):
     count = field.shape[1] - 4 * stride
     result = jnp.zeros((field.shape[0], count, field.shape[2]), jnp.float32)
@@ -51,14 +47,148 @@
     return result
 
 
-def combine_states(first, second):
-    top = jnp.maximum(first[0], second[0])
-    scale_one = jnp.exp(first[0] - top)
-    scale_two = jnp.exp(second[0] - top)
-    rest = tuple(
-        (left * scale_one + right * scale_two for left, right in zip(first[1:], second[1:]))
-    )
-    return (top,) + rest
+def merged_states(logs, means):
+    top = logs[0]
+    for part in logs[1:]:
+        top = jnp.maximum(top, part)
+    weights = [jnp.exp(part - top) for part in logs]
+    total = weights[0]
+    for weight in weights[1:]:
+        total = total + weight
+    colours = []
+    for channel in range(3):
+        colour = weights[0] * means[0][channel]
+        for weight, mean in zip(weights[1:], means[1:]):
+            colour = colour + weight * mean[channel]
+        colours.append(colour / total)
+    return top, total, colours
+
+
+def merge_kernel(
+    logs_ref, means_ref, out_ref,
+    logs_one, means_one, logs_two, means_two, logs_last, means_last,
+    send_sems, recv_sems,
+):
+    place = lax.axis_index("gz")
+    row = place // SIDE
+    col = lax.rem(place, SIDE)
+
+    def peer_of(half, step):
+        if half == 0:
+            return lax.rem(row + step, SIDE) * SIDE + col
+        return row * SIDE + lax.rem(col + step, SIDE)
+
+    barrier = pltpu.get_barrier_semaphore()
+    for half in range(2):
+        for step in range(1, SIDE):
+            pl.semaphore_signal(
+                barrier, inc=1, device_id={"gz": peer_of(half, step)},
+                device_id_type=pl.DeviceIdType.MESH,
+            )
+    pl.semaphore_wait(barrier, 2 * (SIDE - 1))
+
+    def view(ref, half, index):
+        lanes = pl.ds(half * HALF, HALF)
+        if half == 0:
+            return ref.at[index, :, :, lanes] if len(ref.shape) == 4 else ref.at[index, :, :, :, lanes]
+        return ref.at[:, index, :, lanes] if len(ref.shape) == 4 else ref.at[:, index, :, :, lanes]
+
+    def remote(source, target, stage, half, step, kind, peer):
+        return pltpu.make_async_remote_copy(
+            src_ref=source, dst_ref=target,
+            send_sem=send_sems.at[stage, half, step - 1, kind],
+            recv_sem=recv_sems.at[stage, half, step - 1, kind],
+            device_id={"gz": peer}, device_id_type=pl.DeviceIdType.MESH,
+        )
+
+    first = {}
+    for step in (2, 1, 3):
+        for half in range(2):
+            axis_place = row if half == 0 else col
+            index = lax.rem(axis_place + step, SIDE)
+            peer = peer_of(half, step)
+            pair = (
+                remote(view(logs_ref, half, index), logs_one.at[half, step - 1], 0, half, step, 0, peer),
+                remote(view(means_ref, half, index), means_one.at[half, step - 1], 0, half, step, 1, peer),
+            )
+            for copy in pair:
+                copy.start()
+            first[half, step] = pair
+
+    for half in range(2):
+        axis_place = row if half == 0 else col
+        for step in range(1, SIDE):
+            for copy in first[half, step]:
+                copy.wait_recv()
+        own_logs = view(logs_ref, half, axis_place)
+        own_means = view(means_ref, half, axis_place)
+
+        def body(block, carry, half=half, own_logs=own_logs, own_means=own_means):
+            logs = [own_logs[block]] + [logs_one[half, k, block] for k in range(SIDE - 1)]
+            means = [own_means[block].astype(jnp.float32)] + [
+                means_one[half, k, block].astype(jnp.float32) for k in range(SIDE - 1)
+            ]
+            top, total, colours = merged_states(logs, means)
+            logs_two[half, block] = top + jnp.log(total)
+            for channel in range(3):
+                means_two[half, block, channel] = colours[channel].astype(jnp.bfloat16)
+            return carry
+
+        lax.fori_loop(0, SIDE, body, 0)
+
+    second = {}
+    for half in range(2):
+        axis_place = col if half == 0 else row
+        for step in (2, 1, 3):
+            index = lax.rem(axis_place + step, SIDE)
+            peer = peer_of(1 - half, step)
+            pair = (
+                remote(logs_two.at[half, index], logs_last.at[half, step - 1], 1, half, step, 0, peer),
+                remote(means_two.at[half, index], means_last.at[half, step - 1], 1, half, step, 1, peer),
+            )
+            for copy in pair:
+                copy.start()
+            second[half, step] = pair
+
+    for half in range(2):
+        axis_place = col if half == 0 else row
+        for step in range(1, SIDE):
+            for copy in second[half, step]:
+                copy.wait_recv()
+        logs = [logs_two[half, axis_place]] + [logs_last[half, k] for k in range(SIDE - 1)]
+        means = [means_two[half, axis_place].astype(jnp.float32)] + [
+            means_last[half, k].astype(jnp.float32) for k in range(SIDE - 1)
+        ]
+        _, _, colours = merged_states(logs, means)
+        for channel in range(3):
+            out_ref[channel, :, half * HALF : (half + 1) * HALF] = colours[channel].astype(jnp.bfloat16)
+
+    for pair in list(first.values()) + list(second.values()):
+        for copy in pair:
+            copy.wait_send()
+
+
+def merged_bands(logs, means):
+    rows = logs.shape[2]
+    return pl.pallas_call(
+        merge_kernel,
+        out_shape=jax.ShapeDtypeStruct((3, rows, 2 * HALF), jnp.bfloat16),
+        in_specs=[pl.BlockSpec(memory_space=pltpu.VMEM)] * 2,
+        out_specs=pl.BlockSpec(memory_space=pltpu.VMEM),
+        scratch_shapes=[
+            pltpu.VMEM((2, SIDE - 1, SIDE, rows, HALF), jnp.float32),
+            pltpu.VMEM((2, SIDE - 1, SIDE, 3, rows, HALF), jnp.bfloat16),
+            pltpu.VMEM((2, SIDE, rows, HALF), jnp.float32),
+            pltpu.VMEM((2, SIDE, 3, rows, HALF), jnp.bfloat16),
+            pltpu.VMEM((2, SIDE - 1, rows, HALF), jnp.float32),
+            pltpu.VMEM((2, SIDE - 1, 3, rows, HALF), jnp.bfloat16),
+            pltpu.SemaphoreType.DMA((2, 2, SIDE - 1, 2)),
+            pltpu.SemaphoreType.DMA((2, 2, SIDE - 1, 2)),
+        ],
+        compiler_params=pltpu.CompilerParams(
+            collective_id=0, has_side_effects=True, vmem_limit_bytes=32 * 1024 * 1024
+        ),
+    )(logs, means)
 
 
 def per_device(planes, level_gain):
@@ -88,18 +218,16 @@
     local_peak = jnp.max(energy, axis=0)
     weight = jnp.exp(energy - local_peak[None])
     total = jnp.sum(weight, axis=0)
-    colours = tuple(
-        (jnp.sum(weight * planes[:, channel].astype(jnp.float32), axis=0) for channel in range(3))
-    )
     share = rows // lax.axis_size("gz")
-    merged = combined_all((local_peak, total) + colours, "gz", combine_states)
-    start = lax.axis_index("gz") * share
-    band_total = lax.dynamic_slice_in_dim(merged[1], start, share, 0)
-    band_colour = jnp.stack(
-        [lax.dynamic_slice_in_dim(merged[channel + 2], start, share, 0) for channel in range(3)]
-    )
-    joined = (band_colour / band_total[None]).astype(jnp.bfloat16)
-    return joined
+    logs = (local_peak + jnp.log(total)).reshape(SIDE, SIDE, share, -1)
+    means = jnp.stack(
+        [
+            jnp.sum(weight * planes[:, channel].astype(jnp.float32), axis=0) / total
+            for channel in range(3)
+        ]
+    ).astype(jnp.bfloat16)
+    means = means.reshape(3, SIDE, SIDE, share, -1).transpose(1, 2, 0, 3, 4)
+    return merged_bands(logs, means)
 
 
 def solution(mesh):

time: 477 us -> 55 us (0.12)
  the two profiles are of different devices: /device:TPU:1 before, /device:TPU:2 now
where the time goes in v1:
time: 55 us; the launch traced here: 54.9 us
  other arithmetic  23.7 us (43%)
  Pallas kernels  20.3 us (37%)
  starting transfers between devices  5.56 us (10%)
  waiting for transfers between devices  3.12 us (6%)
  local copies, waits for them, and re-layouts  1.96 us (4%)
    pallas_call x1, Pallas kernels, merged_bands(): pl.pallas_call(merge_kernel, out_shape=jax.ShapeDtypeStruct((3, rows, 2 *...  20.3 us
    select_n x3, other arithmetic, per_device(): smoother = jnp.where(inside[None, :, None], smoother, 0.0)  9.37 us
    reduce_max x1, other arithmetic, per_device(): local_peak = jnp.max(energy, axis=0)  5.29 us
    ppermute x1, starting transfers between devices, extended_2(): lax.ppermute(head, axis, [((i + 1) % count, i) for i in range(ends)])  3.64 us
    add x3, other arithmetic, taps_rows(): result = result + factor * field[:, place * stride:place * stride + count]  3.54 us
    convert_element_type x1, other arithmetic, per_device(): luminance = (0.299 * planes[:, 0].astype(jnp.float32) + 0.587 * planes[:,...  2.62 us
    ppermute x1, starting transfers between devices, extended_2(): lax.ppermute(tail, axis, [(i, (i + 1) % count) for i in range(ends)])  1.92 us
    ppermute x1, waiting for transfers between devices, extended_2(): lax.ppermute(head, axis, [((i + 1) % count, i) for i in range(ends)])  1.76 us
  transfers between devices with their start and end apart: 2, of which 2 were waited for; matrix products, arithmetic and copies ran while one was open for 1% of the time, Pallas kernels for 0%

profile of v1, /device:TPU:2, one launch (start us, length us, event | category | flops | bytes accessed | tf_op | source)
XLA Modules:
  0.0 54.9 jit_solution(278780455192842355)
XLA Ops:
  0.0 0.0 copy-start.1
  0.0 2.6 %fusion.51 = bf16[4,128,1024]{2,1,0:T(8,128)(2,1)S(1)} fusion(bf16[4,3,128,1024]{3,2,1,0:T(8,128)(2,1)} %param.2), kind=kLoop, calls=%fused_computation.89 | loop fusion | flops 4718592 | bytes 4194304 | tf_op jit(solution)/shard_map/convert_element_type | solution.py:200
  2.6 0.1 fusion.66
  2.7 1.9 %collective-permute-start = (bf16[4,30,1024]{2,1,0:T(8,128)(2,1)S(1)}, bf16[4,30,1024]{2,1,0:T(8,128)(2,1)S(1)}, u32[]{:S(2)}, u32[]{:S(2)}) collective-permute-start(bf16[4,30,1024]{2,1,0:T(8,128)(2,1)S(1)} %get-tuple-element.13), channel_id=1, source_target_pairs={{0,16},{16,32},{32,48},{48,64},{64,80},{80,96},{96,112},{1,17},{17... | collective-permute-start | bytes 737288 | tf_op jit(solution)/shard_map/ppermute | solution.py:24
  4.6 3.6 %collective-permute-start.1 = (bf16[4,30,1024]{2,1,0:T(8,128)(2,1)S(1)}, bf16[4,30,1024]{2,1,0:T(8,128)(2,1)S(1)}, u32[]{:S(2)}, u32[]{:S(2)}) collective-permute-start(bf16[4,30,1024]{2,1,0:T(8,128)(2,1)S(1)} %get-tuple-element.14), channel_id=1, source_target_pairs={{16,0},{32,16},{48,32},{64,48},{80,64},{96,80},{112,96},{17,1},{33... | collective-permute-start | bytes 737288 | tf_op jit(solution)/shard_map/ppermute | solution.py:26
  8.4 0.0 copy-done.1
  8.4 0.7 %fusion.67 = (f32[1]{0:T(128)}, f32[1]{0:T(128)}, f32[1]{0:T(128)}, f32[1]{0:T(128)}) fusion(f32[4]{0:T(128)S(1)} %copy-done.1), kind=kLoop, calls=%fused_computation.120 | loop fusion | bytes 32 | tf_op jit(solution)/shard_map/slice | solution.py:216
  9.0 1.4 %collective-permute-done = bf16[4,30,1024]{2,1,0:T(8,128)(2,1)S(1)} collective-permute-done((bf16[4,30,1024]{2,1,0:T(8,128)(2,1)S(1)}, bf16[4,30,1024]{2,1,0:T(8,128)(2,1)S(1)}, u32[]{:S(2)}, u32[]{:S(2)}) %collective-permute-start) | collective-permute-done | bytes 245792 | tf_op jit(solution)/shard_map/ppermute | solution.py:24
  10.4 1.8 %collective-permute-done.1 = bf16[4,30,1024]{2,1,0:T(8,128)(2,1)S(1)} collective-permute-done((bf16[4,30,1024]{2,1,0:T(8,128)(2,1)S(1)}, bf16[4,30,1024]{2,1,0:T(8,128)(2,1)S(1)}, u32[]{:S(2)}, u32[]{:S(2)}) %collective-permute-start.1) | collective-permute-done | bytes 245792 | tf_op jit(solution)/shard_map/ppermute | solution.py:26
  12.2 0.4 maximum_convert_fusion
  12.6 0.3 slice.217
  12.9 1.7 %fusion.9 = f32[4,184,1024]{2,1,0:T(8,128)S(1)} fusion(f32[4,188,1024]{2,1,0:T(8,128)S(1)} %maximum_convert_fusion), kind=kLoop, calls=%fused_computation.22 | loop fusion | flops 6782976 | bytes 18087936 | tf_op jit(solution)/shard_map/add | solution.py:37
  14.6 3.4 %fusion.5 = f32[4,184,1024]{2,1,0:T(8,128)S(1)} fusion(f32[4,184,1024]{2,1,0:T(8,128)S(1)} %fusion.9, pred[184]{0:T(512)(128)(4,1)S(1)} %compare_and_fusion.3), kind=kLoop, calls=%fused_computation.17 | loop fusion | flops 7536640 | bytes 6029496 | tf_op jit(solution)/shard_map/jit(_where)/select_n | solution.py:214
  18.0 0.3 slice.218
  18.3 1.3 %fusion.22 = f32[4,176,1024]{2,1,0:T(8,128)S(1)} fusion(f32[4,184,1024]{2,1,0:T(8,128)S(1)} %fusion.5), kind=kLoop, calls=%fused_computation.43 | loop fusion | flops 6488064 | bytes 17301504 | tf_op jit(solution)/shard_map/add | solution.py:37
  19.6 3.2 %fusion.18 = f32[4,176,1024]{2,1,0:T(8,128)S(1)} fusion(f32[4,176,1024]{2,1,0:T(8,128)S(1)} %fusion.22, pred[176]{0:T(512)(128)(4,1)S(1)} %compare_and_fusion.2), kind=kLoop, calls=%fused_computation.38 | loop fusion | flops 7208960 | bytes 5767344 | tf_op jit(solution)/shard_map/jit(_where)/select_n | solution.py:214
  22.8 1.0 %fusion.65 = (f32[4,160,1024]{2,1,0:T(8,128)S(1)}, f32[4,160,1024]{2,1,0:T(8,128)S(1)}) fusion(f32[4,176,1024]{2,1,0:T(8,128)S(1)} %fusion.18), kind=kLoop, calls=%fused_computation.118 | loop fusion | flops 5898240 | bytes 18350080 | tf_op jit(solution)/shard_map/slice | solution.py:216
  23.8 2.8 %fusion.31 = f32[4,160,1024]{2,1,0:T(8,128)S(1)} fusion(f32[4,160,1024]{2,1,0:T(8,128)S(1)} %get-tuple-element.12, pred[160]{0:T(512)(128)(4,1)S(1)} %compare_and_fusion.1), kind=kLoop, calls=%fused_computation.61 | loop fusion | flops 6553600 | bytes 5243040 | tf_op jit(solution)/shard_map/jit(_where)/select_n | solution.py:214
  26.6 0.5 fusion.58
  27.1 0.0 copy-start
  27.1 5.3 %fusion.63 = (f32[128,1024]{1,0:T(8,128)S(1)}, f32[4,128,1024]{2,1,0:T(8,128)S(1)}) fusion(f32[4,128,1024]{2,1,0:T(8,128)S(1)} %fusion.58, pred[128]{0:T(512)(128)(4,1)S(1)} %compare_and_fusion, f32[]{:T(128)} %bitcast.6, f32[4,160,1024]{2,1,0:T(8,128)S(1)} %fusion.31, f32[]{:T(128)} %bitcast.5, f32[4,160,1024]{2,1,0:T(8,128)S(1)} %get-tuple-element.11, ...), kind=kLoop, calls=%fused_computation.117 | loop fusion | flops 13500416 | bytes 13107344 | tf_op jit(solution)/shard_map/reduce_max | solution.py:218
  32.4 0.0 copy-done
  32.5 1.1 %fusion.52 = (f32[128,1024]{1,0:T(8,128)S(1)}, f32[128,1024]{1,0:T(8,128)S(1)}, f32[128,1024]{1,0:T(8,128)S(1)}, f32[128,1024]{1,0:T(8,128)S(1)}) fusion(f32[4,128,1024]{2,1,0:T(8,128)S(1)} %get-tuple-element.10, f32[128,1024]{1,0:T(8,128)S(1)} %get-tuple-element.9, bf16[4,3,128,1024]{3,2,1,0:T(8,128)(2,1)S(1)} %copy-done), kind=kLoop, calls=%fused_computation.90 | loop fusion | flops 5242880 | bytes 7864320 | tf_op jit(solution)/shard_map/reduce_sum | solution.py:225
  33.5 0.3 divide_convert_fusion.2
  33.9 0.1 maximum_bitcast_fusion.means_ref
  33.9 20.3 %shard_map.28 = bf16[3,8,1024]{2,1,0:T(8,128)(2,1)S(1)} custom-call(f32[4,4,8,1024]{3,2,1,0:T(8,128)S(1)} %bitcast.26, bf16[4,4,3,8,1024]{4,3,2,1,0:T(8,128)(2,1)S(1)} %maximum_bitcast_fusion.means_ref), custom_call_target="tpu_custom_call" | custom-call | tf_op jit(solution)/shard_map/pallas_call | solution.py:173
  54.2 0.6 %copy.8 = bf16[3,8,1024]{2,1,0:T(8,128)(2,1)} copy(bf16[3,8,1024]{2,1,0:T(8,128)(2,1)S(1)} %shard_map.28) | data formatting | bytes 98304
  (4 shorter events, 0.0 us)
Async XLA Ops:
  0.0 8.4 %copy-start.1 = (f32[4]{0:T(128)S(1)}, f32[4]{0:T(128)}, u32[]{:S(2)}) copy-start(f32[4]{0:T(128)} %param.3) | copy-start | bytes 52
  2.7 7.7 %collective-permute-start = (bf16[4,30,1024]{2,1,0:T(8,128)(2,1)S(1)}, bf16[4,30,1024]{2,1,0:T(8,128)(2,1)S(1)}, u32[]{:S(2)}, u32[]{:S(2)}) collective-permute-start(bf16[4,30,1024]{2,1,0:T(8,128)(2,1)S(1)} %get-tuple-element.13), channel_id=1, source_target_pairs={{0,16},{16,32},{32,48},{48,64},{64,80},{80,96},{96,112},{1,17},{17... | collective-permute-start | bytes 737288 | tf_op jit(solution)/shard_map/ppermute | solution.py:24
  4.6 7.5 %collective-permute-start.1 = (bf16[4,30,1024]{2,1,0:T(8,128)(2,1)S(1)}, bf16[4,30,1024]{2,1,0:T(8,128)(2,1)S(1)}, u32[]{:S(2)}, u32[]{:S(2)}) collective-permute-start(bf16[4,30,1024]{2,1,0:T(8,128)(2,1)S(1)} %get-tuple-element.14), channel_id=1, source_target_pairs={{16,0},{32,16},{48,32},{64,48},{80,64},{96,80},{112,96},{17,1},{33... | collective-permute-start | bytes 737288 | tf_op jit(solution)/shard_map/ppermute | solution.py:26
  27.1 5.3 %copy-start = (bf16[4,3,128,1024]{3,2,1,0:T(8,128)(2,1)S(1)}, bf16[4,3,128,1024]{3,2,1,0:T(8,128)(2,1)}, u32[]{:S(2)}) copy-start(bf16[4,3,128,1024]{3,2,1,0:T(8,128)(2,1)} %param.2) | copy-start | bytes 9437188

commit v2 on v0

v2 whole, which is shorter than its diff:
```python
import jax
import jax.numpy as jnp
import ml_dtypes
import numpy as np
from jax import lax
from jax.experimental import pallas as pl
from jax.experimental.pallas import tpu as pltpu
from jax.sharding import PartitionSpec as P

LEVELS = 4
TAPS = (0.0625, 0.25, 0.375, 0.25, 0.0625)
SIDE = 4
HALO = 32
LANES = 128
STEPS = (2, 1, 3)
CHAINS = {
    1: ((1, 16),),
    2: ((1, 17), (2, 16)),
    3: ((1, 19), (2, 18), (4, 16)),
    4: ((1, 23), (2, 22), (4, 20), (8, 16)),
}
UNROLL = 2


def column_weights(width):
    composed = np.eye(width)
    pieces = [[], [], []]
    tails = [[], [], []]
    blocks = (0, 1, width // LANES - 1)
    for level in range(LEVELS):
        smooth = np.zeros((width, width))
        for place, factor in enumerate(TAPS):
            smooth += factor * np.eye(width, k=(place - 2) * 2**level)
        composed = smooth @ composed
        scaled = np.pad(composed / 16.0 ** (level + 1), ((0, 0), (64, 64)))
        for variant, block in enumerate(blocks):
            window = scaled[block * LANES : (block + 1) * LANES, block * LANES : block * LANES + 256].T
            head = window.astype(ml_dtypes.bfloat16)
            pieces[variant].append(head)
            if level >= 2:
                tails[variant].append((window - head.astype(np.float64)).astype(ml_dtypes.bfloat16))
    return np.stack([np.concatenate(pieces[v] + tails[v], axis=1) for v in range(3)])


def merged_states(logs, means):
    top = logs[0]
    for part in logs[1:]:
        top = jnp.maximum(top, part)
    weights = [jnp.exp(part - top) for part in logs]
    total = weights[0]
    for weight in weights[1:]:
        total = total + weight
    colours = []
    for channel in range(3):
        colour = weights[0] * means[0][channel]
        for weight, mean in zip(weights[1:], means[1:]):
            colour = colour + weight * mean[channel]
        colours.append(colour / total)
    return top, total, colours


def eight(row):
    return pl.multiple_of(row * 8, 8)


def row_pass(source, target, stride, first, count, outputs):
    def body(index, carry):
        block = index // stride
        base = first + HALO + block * (stride * outputs) + (index - block * stride)
        cells = [source[pl.ds(eight(base + (j - 2) * stride), 8), :] for j in range(outputs + 4)]
        for _ in range(4):
            cells = [left + right for left, right in zip(cells[:-1], cells[1:])]
        for j in range(outputs):
            target[pl.ds(eight(base + j * stride), 8), :] = cells[j]
        return carry

    lax.fori_loop(0, count // outputs, body, 0, unroll=UNROLL)


def focus_kernel(
    gain_ref, planes_hbm, weights_hbm, out_ref,
    planes, weights, lum, field, smooth, buf_a, buf_b, score,
    logs_zero, means_zero, logs_one, means_one, logs_two, means_two, logs_last, means_last,
    load_sems, halo_send, halo_recv, send_sems, recv_sems,
):
    tile = lax.axis_index("tile")
    tiles = lax.axis_size("tile")
    place = lax.axis_index("gz")
    row = place // SIDE
    col = lax.rem(place, SIDE)
    rows = planes.shape[2]
    width = planes.shape[3]
    pairs = width // (2 * LANES)
    quarter = rows // SIDE
    extent = rows + 2 * HALO

    def peer_of(half, step):
        if half == 0:
            return lax.rem(row + step, SIDE) * SIDE + col
        return row * SIDE + lax.rem(col + step, SIDE)

    barrier = pltpu.get_barrier_semaphore()
    for half in range(2):
        for step in range(1, SIDE):
            pl.semaphore_signal(
                barrier, inc=1, device_id={"gz": peer_of(half, step)},
                device_id_type=pl.DeviceIdType.MESH,
            )

    @pl.when(tile > 0)
    def _():
        pl.semaphore_signal(
            barrier, inc=1, device_id={"tile": tile - 1}, device_id_type=pl.DeviceIdType.MESH
        )

    @pl.when(tile < tiles - 1)
    def _():
        pl.semaphore_signal(
            barrier, inc=1, device_id={"tile": tile + 1}, device_id_type=pl.DeviceIdType.MESH
        )

    loads = [
        pltpu.make_async_copy(
            planes_hbm.at[:, :, pl.ds(q * quarter, quarter), :],
            planes.at[:, :, pl.ds(q * quarter, quarter), :],
            load_sems.at[q],
        )
        for q in range(SIDE)
    ]
    weight_load = pltpu.make_async_copy(weights_hbm, weights, load_sems.at[SIDE])
    for q in (0, 3, 1, 2):
        loads[q].start()
    weight_load.start()

    def luminance(q):
        def body(index, carry):
            plane = index // 2
            start = pl.multiple_of(q * quarter + (index - plane * 2) * 16, 16)
            cells = [planes[plane, c, pl.ds(start, 16), :].astype(jnp.float32) for c in range(3)]
            value = (0.299 * cells[0] + 0.587 * cells[1] + 0.114 * cells[2]).astype(jnp.bfloat16)
            value = value.astype(jnp.float32)
            for k in range(width // LANES):
                field[k // 2, pl.ds(start * 8 + plane * 2 + k % 2, 16, stride=8), :] = value[
                    :, k * LANES : (k + 1) * LANES
                ]
            wide = jnp.concatenate([value, jnp.zeros((16, LANES), jnp.float32)], axis=1)
            wide = pltpu.roll(wide, LANES // 2, axis=1).astype(jnp.bfloat16)
            lum[plane, pl.ds(pl.multiple_of(start + HALO, 16), 16), :] = wide
            return carry

        lax.fori_loop(0, 8, body, 0)

    def halo_copy(side):
        source = HALO if side == 0 else rows
        target = HALO + rows if side == 0 else 0
        peer = tile - 1 if side == 0 else tile + 1
        return pltpu.make_async_remote_copy(
            src_ref=lum.at[:, pl.ds(source, HALO), :],
            dst_ref=lum.at[:, pl.ds(target, HALO), :],
            send_sem=halo_send.at[side], recv_sem=halo_recv.at[side],
            device_id={"tile": peer}, device_id_type=pl.DeviceIdType.MESH,
        )

    loads[0].wait()
    luminance(0)
    neighbours = jnp.where(tile > 0, 1, 0) + jnp.where(tile < tiles - 1, 1, 0)
    pl.semaphore_wait(barrier, 2 * (SIDE - 1) + neighbours)

    @pl.when(tile > 0)
    def _():
        halo_copy(0).start()

    @pl.when(tile == 0)
    def _():
        lum[:, 0:HALO, :] = jnp.zeros((SIDE, HALO, width + LANES), jnp.bfloat16)

    loads[3].wait()
    luminance(3)

    @pl.when(tile < tiles - 1)
    def _():
        halo_copy(1).start()

    @pl.when(tile == tiles - 1)
    def _():
        lum[:, HALO + rows : extent, :] = jnp.zeros((SIDE, HALO, width + LANES), jnp.bfloat16)

    for q in (1, 2):
        loads[q].wait()
        luminance(q)
    weight_load.wait()

    def columns(pair, spans):
        for k in range(2):
            block = pair * 2 + k
            variant = jnp.where(block == 0, 0, jnp.where(block == 2 * pairs - 1, 2, 1))
            window = pl.ds(pl.multiple_of(block * LANES, LANES), 2 * LANES)
            cells = jnp.concatenate(
                [
                    lum[plane, start : start + count, window]
                    for plane in range(SIDE)
                    for start, count in spans
                ],
                axis=0,
            )
            low = jnp.dot(cells, weights[variant, :, 0:256], preferred_element_type=jnp.float32)
            high = jnp.dot(
                cells, weights[variant, :, 256:512], preferred_element_type=jnp.float32
            ) + jnp.dot(cells, weights[variant, :, 512:768], preferred_element_type=jnp.float32)
            at = 0
            for plane in range(SIDE):
                for start, count in spans:
                    spot = pl.ds(start * 8 + plane * 2 + k, count, stride=8)
                    part = slice(at, at + count)
                    smooth[pair, 0, spot, :] = low[part, :LANES]
                    smooth[pair, 1, spot, :] = low[part, LANES:]
                    smooth[pair, 2, spot, :] = high[part, :LANES]
                    smooth[pair, 3, spot, :] = high[part, LANES:]
                    at += count

    def inner_columns(pair, carry):
        columns(pair, ((HALO, rows),))
        return carry

    lax.fori_loop(0, pairs, inner_columns, 0)

    @pl.when(tile < tiles - 1)
    def _():
        halo_copy(0).wait_recv()

    @pl.when(tile > 0)
    def _():
        halo_copy(1).wait_recv()

    def zero_outside(target, reach):
        blank = jnp.zeros((reach * 8, LANES), jnp.float32)

        @pl.when(tile == 0)
        def _():
            target[(HALO - reach) * 8 : HALO * 8, :] = blank

        @pl.when(tile == tiles - 1)
        def _():
            target[(HALO + rows) * 8 : (HALO + rows + reach) * 8, :] = blank

    def rows_smoothed(pair):
        for level in range(LEVELS, 0, -1):
            chain = CHAINS[level]
            reach = sum(2 * stride for stride, _ in chain)
            own = smooth.at[pair, level - 1]
            source = own
            for index, (stride, outputs) in enumerate(chain):
                reach -= 2 * stride
                target = (buf_a, buf_b)[index % 2]
                if index == level - 1 and level > 1:
                    target = own
                row_pass(source, target, stride, -reach, rows + 2 * reach, outputs)
                if reach:
                    zero_outside(target, reach)
                source = target

    gains = [gain_ref[level] for level in range(LEVELS)]

    def scored(pair):
        def body(block, carry):
            here = pl.ds(pl.multiple_of(block * 64, 64), 64)
            wide = pl.ds(pl.multiple_of(block * 64 + HALO * 8, 64), 64)
            approx = [field[pair, here, :], buf_a[wide, :]]
            approx += [smooth[pair, level, wide, :] for level in range(1, LEVELS)]
            energy = None
            for level in range(LEVELS):
                detail = approx[level] - approx[level + 1]
                term = gains[level] * (detail * detail)
                energy = term if energy is None else energy + term
            score[here, :] = energy
            return carry

        lax.fori_loop(0, rows // 8, body, 0)

    def states(pair):
        def body(block, carry):
            here = pl.ds(pl.multiple_of(block * 16, 16), 16)
            far = block // 2
            near = (block - far * 2) * 2
            for k in range(2):
                lanes = pl.ds(pl.multiple_of((pair * 2 + k) * LANES, LANES), LANES)
                parts = [
                    score[pl.ds(block * 128 + plane * 2 + k, 16, stride=8), :] for plane in range(SIDE)
                ]
                top = jnp.maximum(jnp.maximum(parts[0], parts[1]), jnp.maximum(parts[2], parts[3]))
                shares = [jnp.exp(part - top) for part in parts]
                total = (shares[0] + shares[1]) + (shares[2] + shares[3])
                inverse = 1.0 / total
                shares = [share * inverse for share in shares]
                log_sum = top + jnp.log(total)
                spots = ((far, near), (far, near + 1)) if k == 0 else ((near, far), (near + 1, far))
                for part, (first, second) in enumerate(spots):
                    logs_zero[pair, k, first, second] = log_sum[part * 8 : part * 8 + 8]
                for channel in range(3):
                    mean = shares[0] * planes[0, channel, here, lanes].astype(jnp.float32)
                    for plane in range(1, SIDE):
                        mean = mean + shares[plane] * planes[plane, channel, here, lanes].astype(
                            jnp.float32
                        )
                    mean = mean.astype(jnp.bfloat16)
                    for part, (first, second) in enumerate(spots):
                        means_zero[pair, k, first, second, channel] = mean[part * 8 : part * 8 + 8]
            return carry

        lax.fori_loop(0, rows // 16, body, 0)

    def first_copies(pair, half, step):
        index = lax.rem((row if half == 0 else col) + step, SIDE)
        return [
            pltpu.make_async_remote_copy(
                src_ref=source.at[pair, half, index], dst_ref=target.at[pair, half, step - 1],
                send_sem=send_sems.at[pair, half, step - 1, kind],
                recv_sem=recv_sems.at[pair, half, step - 1, kind],
                device_id={"gz": peer_of(half, step)}, device_id_type=pl.DeviceIdType.MESH,
            )
            for kind, (source, target) in enumerate(
                ((logs_zero, logs_one), (means_zero, means_one))
            )
        ]

    def first_merge(pair):
        for half in range(2):
            own = row if half == 0 else col
            for step in STEPS:
                for copy in first_copies(pair, half, step):
                    copy.wait_recv()

            def body(second, carry, half=half, own=own):
                logs = [logs_zero[pair, half, own, second]]
                logs += [logs_one[pair, half, k, second] for k in range(SIDE - 1)]
                means = [means_zero[pair, half, own, second].astype(jnp.float32)]
                means += [
                    means_one[pair, half, k, second].astype(jnp.float32) for k in range(SIDE - 1)
                ]
                top, total, colours = merged_states(logs, means)
                logs_two[half, second, pair] = top + jnp.log(total)
                for channel in range(3):
                    means_two[half, second, pair, channel] = colours[channel].astype(jnp.bfloat16)
                return carry

            lax.fori_loop(0, SIDE, body, 0)

    def one_pair(pair, carry):
        columns(pair, ((0, HALO), (HALO + rows, HALO)))
        rows_smoothed(pair)
        scored(pair)
        states(pair)
        for step in STEPS:
            for half in range(2):
                for copy in first_copies(pair, half, step):
                    copy.start()

        @pl.when(pair > 0)
        def _():
            first_merge(pair - 1)

        return carry

    lax.fori_loop(0, pairs, one_pair, 0)
    first_merge(pairs - 1)

    def last_copies(half, step):
        index = lax.rem((col if half == 0 else row) + step, SIDE)
        return [
            pltpu.make_async_remote_copy(
                src_ref=source.at[half, index], dst_ref=target.at[half, step - 1],
                send_sem=send_sems.at[pairs, half, step - 1, kind],
                recv_sem=recv_sems.at[pairs, half, step - 1, kind],
                device_id={"gz": peer_of(1 - half, step)}, device_id_type=pl.DeviceIdType.MESH,
            )
            for kind, (source, target) in enumerate(((logs_two, logs_last), (means_two, means_last)))
        ]

    for step in STEPS:
        for half in range(2):
            for copy in last_copies(half, step):
                copy.start()

    for half in range(2):
        own = col if half == 0 else row
        for step in STEPS:
            for copy in last_copies(half, step):
                copy.wait_recv()
        for pair in range(pairs):
            logs = [logs_two[half, own, pair]] + [logs_last[half, k, pair] for k in range(SIDE - 1)]
            means = [means_two[half, own, pair].astype(jnp.float32)]
            means += [means_last[half, k, pair].astype(jnp.float32) for k in range(SIDE - 1)]
            _, _, colours = merged_states(logs, means)
            lanes = slice((pair * 2 + half) * LANES, (pair * 2 + half + 1) * LANES)
            for channel in range(3):
                out_ref[channel, :, lanes] = colours[channel].astype(jnp.bfloat16)

    @pl.when(tile > 0)
    def _():
        halo_copy(0).wait_send()

    @pl.when(tile < tiles - 1)
    def _():
        halo_copy(1).wait_send()

    def drain(pair, carry):
        for half in range(2):
            for step in STEPS:
                for copy in first_copies(pair, half, step):
                    copy.wait_send()
        return carry

    lax.fori_loop(0, pairs, drain, 0)
    for half in range(2):
        for step in STEPS:
            for copy in last_copies(half, step):
                copy.wait_send()


def per_device(planes, level_gain):
    _, channels, rows, width = planes.shape
    share = rows // (SIDE * SIDE)
    pairs = width // (2 * LANES)
    extent = rows + 2 * HALO
    weights = jnp.asarray(column_weights(width))
    others = SIDE - 1
    return pl.pallas_call(
        focus_kernel,
        out_shape=jax.ShapeDtypeStruct((channels, share, width), jnp.bfloat16),
        in_specs=[
            pl.BlockSpec(memory_space=pltpu.SMEM),
            pl.BlockSpec(memory_space=pl.ANY),
            pl.BlockSpec(memory_space=pl.ANY),
        ],
        out_specs=pl.BlockSpec(memory_space=pltpu.VMEM),
        scratch_shapes=[
            pltpu.VMEM(planes.shape, jnp.bfloat16),
            pltpu.VMEM(weights.shape, jnp.bfloat16),
            pltpu.VMEM((SIDE, extent, width + LANES), jnp.bfloat16),
            pltpu.VMEM((pairs, rows * 8, LANES), jnp.float32),
            pltpu.VMEM((pairs, LEVELS, extent * 8, LANES), jnp.float32),
            pltpu.VMEM((extent * 8, LANES), jnp.float32),
            pltpu.VMEM((extent * 8, LANES), jnp.float32),
            pltpu.VMEM((rows * 8, LANES), jnp.float32),
            pltpu.VMEM((pairs, 2, SIDE, SIDE, share, LANES), jnp.float32),
            pltpu.VMEM((pairs, 2, SIDE, SIDE, channels, share, LANES), jnp.bfloat16),
            pltpu.VMEM((pairs, 2, others, SIDE, share, LANES), jnp.float32),
            pltpu.VMEM((pairs, 2, others, SIDE, channels, share, LANES), jnp.bfloat16),
            pltpu.VMEM((2, SIDE, pairs, share, LANES), jnp.float32),
            pltpu.VMEM((2, SIDE, pairs, channels, share, LANES), jnp.bfloat16),
            pltpu.VMEM((2, others, pairs, share, LANES), jnp.float32),
            pltpu.VMEM((2, others, pairs, channels, share, LANES), jnp.bfloat16),
            pltpu.SemaphoreType.DMA((SIDE + 1,)),
            pltpu.SemaphoreType.DMA((2,)),
            pltpu.SemaphoreType.DMA((2,)),
            pltpu.SemaphoreType.DMA((pairs + 1, 2, others, 2)),
            pltpu.SemaphoreType.DMA((pairs + 1, 2, others, 2)),
        ],
        compiler_params=pltpu.CompilerParams(
            collective_id=0, has_side_effects=True, vmem_limit_bytes=50 * 1024 * 1024
        ),
    )(level_gain, planes, weights)


def solution(mesh):
    return jax.shard_map(
        per_device,
        mesh=mesh,
        in_specs=(P("gz", None, "tile", None), P()),
        out_specs=P(None, ("tile", "gz"), None),
        check_vma=False,
    )
```

time: 477 us -> 38.2 us (0.08)
  waiting for transfers between devices: 332 us -> 0 us
  other arithmetic: 82.8 us -> 0 us
  local copies, waits for them, and re-layouts: 41 us -> 2.55 us
  Pallas kernels: 0 us -> 35.5 us
  between operations: 13.4 us -> 0.01 us
  starting transfers between devices: 6.77 us -> 0 us
    all_gather x5 -> x0, waiting for transfers between devices: 325 us -> none  [combined_all(): pieces = jax.tree.map(lambda part: lax.all_gather(part, axis), value)]
    add x33 -> x0, other arithmetic: 57.2 us -> none  [the longest x30 53.7 us: combine_states(): left * scale_one + right * scale_two]
    slice x19 -> x0, local copies, waits for them, and re-layouts: 41 us -> none  [the longest x5 39.7 us: combined_all(): tail = jax.tree.map(lambda part: part[1:], pieces)]
    pallas_call x0 -> x1, Pallas kernels: none -> 35.5 us  [per_device(): pl.pallas_call(focus_kernel, out_shape=jax.ShapeDtypeStruct((channels, sh...]
    select_n x3 -> x0, other arithmetic: 9.37 us -> none  [per_device(): smoother = jnp.where(inside[None, :, None], smoother, 0.0)]
    reduce_max x1 -> x0, other arithmetic: 7.27 us -> none  [per_device(): local_peak = jnp.max(energy, axis=0)]
    ppermute x2 -> x0, starting transfers between devices: 6.43 us -> none  [the longest x1 4.51 us: extended_2(): lax.ppermute(tail, axis, [(i, (i + 1) % count) for i in range(ends)])]
    ppermute x2 -> x0, waiting for transfers between devices: 5.01 us -> none  [the longest x1 4.4 us: extended_2(): lax.ppermute(head, axis, [((i + 1) % count, i) for i in range(ends)])]
  transfers between devices with their start and end apart: 7 -> 0, of which waited for: 7 -> 0; matrix products, arithmetic and copies ran while one was open for 8% -> 0% of each run, Pallas kernels for 0% -> 0%
where the time goes in v2:
time: 38.2 us; the launch traced here: 38 us
  Pallas kernels  35.5 us (93%)
  local copies, waits for them, and re-layouts  2.55 us (7%)
    pallas_call x1, Pallas kernels, per_device(): pl.pallas_call(focus_kernel, out_shape=jax.ShapeDtypeStruct((channels, sh...  35.5 us
    unnamed x5, local copies, waits for them, and re-layouts  2.55 us

profile of v2, /device:TPU:1, one launch (start us, length us, event | category | flops | bytes accessed | tf_op | source)
XLA Modules:
  0.0 38.0 jit_solution(4457436801351961412)
XLA Ops:
  0.0 0.0 copy-start
  0.0 1.3 %copy-done = bf16[3,256,768]{2,1,0:T(8,128)(2,1)S(1)} copy-done((bf16[3,256,768]{2,1,0:T(8,128)(2,1)S(1)}, bf16[3,256,768]{2,1,0:T(8,128)(2,1)}, u32[]{:S(2)}) %copy-start) | copy-done | bytes 1179672
  1.3 0.0 copy-start.1
  1.3 0.7 %copy-done.1 = f32[4]{0:T(128)S(1)} copy-done((f32[4]{0:T(128)S(1)}, f32[4]{0:T(128)}, u32[]{:S(2)}) %copy-start.1) | copy-done | bytes 40
  1.9 35.5 %shard_map.37 = bf16[3,8,1024]{2,1,0:T(8,128)(2,1)S(1)} custom-call(f32[4]{0:T(128)S(1)} %copy-done.1, bf16[4,3,128,1024]{3,2,1,0:T(8,128)(2,1)} %planes_hbm.1, bf16[3,256,768]{2,1,0:T(8,128)(2,1)S(1)} %copy-done), custom_call_target="tpu_custom_call" | custom-call | tf_op jit(solution)/shard_map/pallas_call | solution.py:427
  37.4 0.6 %copy.5 = bf16[3,8,1024]{2,1,0:T(8,128)(2,1)} copy(bf16[3,8,1024]{2,1,0:T(8,128)(2,1)S(1)} %shard_map.37) | data formatting | bytes 98304
Async XLA Ops:
  0.0 1.3 %copy-start = (bf16[3,256,768]{2,1,0:T(8,128)(2,1)S(1)}, bf16[3,256,768]{2,1,0:T(8,128)(2,1)}, u32[]{:S(2)}) copy-start(bf16[3,256,768]{2,1,0:T(8,128)(2,1)} %constant.2.clone.weights_hbm) | copy-start | bytes 3538948
  1.3 0.7 %copy-start.1 = (f32[4]{0:T(128)S(1)}, f32[4]{0:T(128)}, u32[]{:S(2)}) copy-start(f32[4]{0:T(128)} %gain_ref.1) | copy-start | bytes 52

commit v3 on v2

--- a/solution.py
+++ b/solution.py
@@ -19,7 +19,9 @@
     3: ((1, 19), (2, 18), (4, 16)),
     4: ((1, 23), (2, 22), (4, 20), (8, 16)),
 }
-UNROLL = 2
+UNROLL_LUM = 2
+UNROLL_SCORE = 2
+UNROLL_STATES = 2
 
 
 def column_weights(width):
@@ -59,22 +61,20 @@
     return top, total, colours
 
 
-def eight(row):
-    return pl.multiple_of(row * 8, 8)
-
-
-def row_pass(source, target, stride, first, count, outputs):
-    def body(index, carry):
-        block = index // stride
-        base = first + HALO + block * (stride * outputs) + (index - block * stride)
-        cells = [source[pl.ds(eight(base + (j - 2) * stride), 8), :] for j in range(outputs + 4)]
-        for _ in range(4):
-            cells = [left + right for left, right in zip(cells[:-1], cells[1:])]
-        for j in range(outputs):
-            target[pl.ds(eight(base + j * stride), 8), :] = cells[j]
-        return carry
-
-    lax.fori_loop(0, count // outputs, body, 0, unroll=UNROLL)
+def row_pass(source, target, stride, reach, rows, outputs, keep):
+    for start in range(-reach, rows + reach, stride * outputs):
+        for base in range(start, start + stride):
+            at = [(base + HALO + (j - 2) * stride) * 8 for j in range(outputs + 4)]
+            cells = [source[spot : spot + 8, :] for spot in at]
+            for _ in range(4):
+                cells = [left + right for left, right in zip(cells[:-1], cells[1:])]
+            for j, cell in enumerate(cells):
+                place = base + j * stride
+                if place < 0:
+                    cell = cell * keep[0]
+                if place >= rows:
+                    cell = cell * keep[1]
+                target[at[j + 2] : at[j + 2] + 8, :] = cell
 
 
 def focus_kernel(
@@ -148,7 +148,7 @@
             lum[plane, pl.ds(pl.multiple_of(start + HALO, 16), 16), :] = wide
             return carry
 
-        lax.fori_loop(0, 8, body, 0)
+        lax.fori_loop(0, 8, body, 0, unroll=UNROLL_LUM)
 
     def halo_copy(side):
         source = HALO if side == 0 else rows
@@ -205,8 +205,10 @@
             )
             low = jnp.dot(cells, weights[variant, :, 0:256], preferred_element_type=jnp.float32)
             high = jnp.dot(
-                cells, weights[variant, :, 256:512], preferred_element_type=jnp.float32
-            ) + jnp.dot(cells, weights[variant, :, 512:768], preferred_element_type=jnp.float32)
+                jnp.concatenate([cells, cells], axis=1),
+                jnp.concatenate([weights[variant, :, 256:512], weights[variant, :, 512:768]], axis=0),
+                preferred_element_type=jnp.float32,
+            )
             at = 0
             for plane in range(SIDE):
                 for start, count in spans:
@@ -232,16 +234,7 @@
     def _():
         halo_copy(1).wait_recv()
 
-    def zero_outside(target, reach):
-        blank = jnp.zeros((reach * 8, LANES), jnp.float32)
-
-        @pl.when(tile == 0)
-        def _():
-            target[(HALO - reach) * 8 : HALO * 8, :] = blank
-
-        @pl.when(tile == tiles - 1)
-        def _():
-            target[(HALO + rows) * 8 : (HALO + rows + reach) * 8, :] = blank
+    keep = (jnp.where(tile == 0, 0.0, 1.0), jnp.where(tile == tiles - 1, 0.0, 1.0))
 
     def rows_smoothed(pair):
         for level in range(LEVELS, 0, -1):
@@ -254,9 +247,7 @@
                 target = (buf_a, buf_b)[index % 2]
                 if index == level - 1 and level > 1:
                     target = own
-                row_pass(source, target, stride, -reach, rows + 2 * reach, outputs)
-                if reach:
-                    zero_outside(target, reach)
+                row_pass(source, target, stride, reach, rows, outputs, keep)
                 source = target
 
     gains = [gain_ref[level] for level in range(LEVELS)]
@@ -275,7 +266,7 @@
             score[here, :] = energy
             return carry
 
-        lax.fori_loop(0, rows // 8, body, 0)
+        lax.fori_loop(0, rows // 8, body, 0, unroll=UNROLL_SCORE)
 
     def states(pair):
         def body(block, carry):
@@ -307,7 +298,7 @@
                         means_zero[pair, k, first, second, channel] = mean[part * 8 : part * 8 + 8]
             return carry
 
-        lax.fori_loop(0, rows // 16, body, 0)
+        lax.fori_loop(0, rows // 16, body, 0, unroll=UNROLL_STATES)
 
     def first_copies(pair, half, step):
         index = lax.rem((row if half == 0 else col) + step, SIDE)
@@ -330,7 +321,7 @@
                 for copy in first_copies(pair, half, step):
                     copy.wait_recv()
 
-            def body(second, carry, half=half, own=own):
+            for second in range(SIDE):
                 logs = [logs_zero[pair, half, own, second]]
                 logs += [logs_one[pair, half, k, second] for k in range(SIDE - 1)]
                 means = [means_zero[pair, half, own, second].astype(jnp.float32)]
@@ -338,12 +329,9 @@
                     means_one[pair, half, k, second].astype(jnp.float32) for k in range(SIDE - 1)
                 ]
                 top, total, colours = merged_states(logs, means)
-                logs_two[half, second, pair] = top + jnp.log(total)
+                logs_two[pair, half, second] = top + jnp.log(total)
                 for channel in range(3):
-                    means_two[half, second, pair, channel] = colours[channel].astype(jnp.bfloat16)
-                return carry
-
-            lax.fori_loop(0, SIDE, body, 0)
+                    means_two[pair, half, second, channel] = colours[channel].astype(jnp.bfloat16)
 
     def one_pair(pair, carry):
         columns(pair, ((0, HALO), (HALO + rows, HALO)))
@@ -355,46 +343,51 @@
                 for copy in first_copies(pair, half, step):
                     copy.start()
 
-        @pl.when(pair > 0)
+        @pl.when(pair > 1)
         def _():
-            first_merge(pair - 1)
+            advance(pair - 2)
 
         return carry
 
-    lax.fori_loop(0, pairs, one_pair, 0)
-    first_merge(pairs - 1)
-
-    def last_copies(half, step):
+    def advance(pair):
+        first_merge(pair)
+        for step in STEPS:
+            for half in range(2):
+                for copy in last_copies(pair, half, step):
+                    copy.start()
+
+    def last_copies(pair, half, step):
         index = lax.rem((col if half == 0 else row) + step, SIDE)
         return [
             pltpu.make_async_remote_copy(
-                src_ref=source.at[half, index], dst_ref=target.at[half, step - 1],
-                send_sem=send_sems.at[pairs, half, step - 1, kind],
-                recv_sem=recv_sems.at[pairs, half, step - 1, kind],
+                src_ref=source.at[pair, half, index], dst_ref=target.at[pair, half, step - 1],
+                send_sem=send_sems.at[pairs + pair, half, step - 1, kind],
+                recv_sem=recv_sems.at[pairs + pair, half, step - 1, kind],
                 device_id={"gz": peer_of(1 - half, step)}, device_id_type=pl.DeviceIdType.MESH,
             )
             for kind, (source, target) in enumerate(((logs_two, logs_last), (means_two, means_last)))
         ]
 
-    for step in STEPS:
+    def last_merge(pair):
         for half in range(2):
-            for copy in last_copies(half, step):
-                copy.start()
-
-    for half in range(2):
-        own = col if half == 0 else row
-        for step in STEPS:
-            for copy in last_copies(half, step):
-                copy.wait_recv()
-        for pair in range(pairs):
-            logs = [logs_two[half, own, pair]] + [logs_last[half, k, pair] for k in range(SIDE - 1)]
-            means = [means_two[half, own, pair].astype(jnp.float32)]
-            means += [means_last[half, k, pair].astype(jnp.float32) for k in range(SIDE - 1)]
+            own = col if half == 0 else row
+            for step in STEPS:
+                for copy in last_copies(pair, half, step):
+                    copy.wait_recv()
+            logs = [logs_two[pair, half, own]] + [logs_last[pair, half, k] for k in range(SIDE - 1)]
+            means = [means_two[pair, half, own].astype(jnp.float32)]
+            means += [means_last[pair, half, k].astype(jnp.float32) for k in range(SIDE - 1)]
             _, _, colours = merged_states(logs, means)
             lanes = slice((pair * 2 + half) * LANES, (pair * 2 + half + 1) * LANES)
             for channel in range(3):
                 out_ref[channel, :, lanes] = colours[channel].astype(jnp.bfloat16)
 
+    lax.fori_loop(0, pairs, one_pair, 0)
+    advance(pairs - 2)
+    advance(pairs - 1)
+    for pair in range(pairs):
+        last_merge(pair)
+
     @pl.when(tile > 0)
     def _():
         halo_copy(0).wait_send()
@@ -406,15 +399,11 @@
     def drain(pair, carry):
         for half in range(2):
             for step in STEPS:
-                for copy in first_copies(pair, half, step):
+                for copy in first_copies(pair, half, step) + last_copies(pair, half, step):
                     copy.wait_send()
         return carry
 
     lax.fori_loop(0, pairs, drain, 0)
-    for half in range(2):
-        for step in STEPS:
-            for copy in last_copies(half, step):
-                copy.wait_send()
 
 
 def per_device(planes, level_gain):
@@ -446,18 +435,18 @@
             pltpu.VMEM((pairs, 2, SIDE, SIDE, channels, share, LANES), jnp.bfloat16),
             pltpu.VMEM((pairs, 2, others, SIDE, share, LANES), jnp.float32),
             pltpu.VMEM((pairs, 2, others, SIDE, channels, share, LANES), jnp.bfloat16),
-            pltpu.VMEM((2, SIDE, pairs, share, LANES), jnp.float32),
-            pltpu.VMEM((2, SIDE, pairs, channels, share, LANES), jnp.bfloat16),
-            pltpu.VMEM((2, others, pairs, share, LANES), jnp.float32),
-            pltpu.VMEM((2, others, pairs, channels, share, LANES), jnp.bfloat16),
+            pltpu.VMEM((pairs, 2, SIDE, share, LANES), jnp.float32),
+            pltpu.VMEM((pairs, 2, SIDE, channels, share, LANES), jnp.bfloat16),
+            pltpu.VMEM((pairs, 2, others, share, LANES), jnp.float32),
+            pltpu.VMEM((pairs, 2, others, channels, share, LANES), jnp.bfloat16),
             pltpu.SemaphoreType.DMA((SIDE + 1,)),
             pltpu.SemaphoreType.DMA((2,)),
             pltpu.SemaphoreType.DMA((2,)),
-            pltpu.SemaphoreType.DMA((pairs + 1, 2, others, 2)),
-            pltpu.SemaphoreType.DMA((pairs + 1, 2, others, 2)),
+            pltpu.SemaphoreType.DMA((2 * pairs, 2, others, 2)),
+            pltpu.SemaphoreType.DMA((2 * pairs, 2, others, 2)),
         ],
         compiler_params=pltpu.CompilerParams(
-            collective_id=0, has_side_effects=True, vmem_limit_bytes=50 * 1024 * 1024
+            collective_id=0, has_side_effects=True, vmem_limit_bytes=60 * 1024 * 1024
         ),
     )(level_gain, planes, weights)
 

time: 38.2 us -> 32.3 us (0.85); the launches traced: 38 us -> 31.7 us
  Pallas kernels: 35.5 us -> 30.2 us
  local copies, waits for them, and re-layouts: 2.55 us -> 1.42 us
    pallas_call x1, Pallas kernels: 35.5 us -> 30.2 us  [per_device(): pl.pallas_call(focus_kernel, out_shape=jax.ShapeDtypeStruct((channels, sh...]
    unnamed x5 -> x1, local copies, waits for them, and re-layouts: 2.55 us -> 1.42 us
where the time goes in v3:
time: 32.3 us; the launch traced here: 31.7 us
  Pallas kernels  30.2 us (93%)
  local copies, waits for them, and re-layouts  1.42 us (4%)
    pallas_call x1, Pallas kernels, per_device(): pl.pallas_call(focus_kernel, out_shape=jax.ShapeDtypeStruct((channels, sh...  30.2 us
    unnamed x1, local copies, waits for them, and re-layouts  1.42 us

profile of v3, /device:TPU:1, one launch (start us, length us, event | category | flops | bytes accessed | tf_op | source)
XLA Modules:
  0.0 31.7 jit_solution(5318881405362414725)
XLA Ops:
  0.0 30.2 %shard_map.37 = bf16[3,8,1024]{2,1,0:T(8,128)(2,1)} custom-call(f32[4]{0:T(128)} %gain_ref.1, bf16[4,3,128,1024]{3,2,1,0:T(8,128)(2,1)} %planes_hbm.1, bf16[3,256,768]{2,1,0:T(8,128)(2,1)} %constant.2.clone.weights_hbm), custom_call_target="tpu_custom_call" | custom-call | tf_op jit(solution)/shard_map/pallas_call | solution.py:416
  30.3 1.4 %copy.5 = bf16[3,8,1024]{2,1,0:T(8,128)(2,1)} copy(bf16[3,8,1024]{2,1,0:T(8,128)(2,1)} %shard_map.37) | data formatting | bytes 98304

commit v4 on v3

--- a/solution.py
+++ b/solution.py
@@ -19,6 +19,7 @@
     3: ((1, 19), (2, 18), (4, 16)),
     4: ((1, 23), (2, 22), (4, 20), (8, 16)),
 }
+AHEAD = 3
 UNROLL_LUM = 2
 UNROLL_SCORE = 2
 UNROLL_STATES = 2
@@ -79,10 +80,11 @@
 
 def focus_kernel(
     gain_ref, planes_hbm, weights_hbm, out_ref,
-    planes, weights, lum, field, smooth, buf_a, buf_b, score,
+    planes, weights, lum, field, smooth_0, smooth_1, smooth_2, smooth_3, buf_a, buf_b, score,
     logs_zero, means_zero, logs_one, means_one, logs_two, means_two, logs_last, means_last,
     load_sems, halo_send, halo_recv, send_sems, recv_sems,
 ):
+    smooths = (smooth_0, smooth_1, smooth_2, smooth_3)
     tile = lax.axis_index("tile")
     tiles = lax.axis_size("tile")
     place = lax.axis_index("gz")
@@ -150,14 +152,16 @@
 
         lax.fori_loop(0, 8, body, 0, unroll=UNROLL_LUM)
 
-    def halo_copy(side):
+    def halo_copy(side, part):
         source = HALO if side == 0 else rows
         target = HALO + rows if side == 0 else 0
         peer = tile - 1 if side == 0 else tile + 1
+        first = 0 if part == 0 else (2 * part + 1) * LANES
+        lanes = pl.ds(first, (2 * part + 3) * LANES - first)
         return pltpu.make_async_remote_copy(
-            src_ref=lum.at[:, pl.ds(source, HALO), :],
-            dst_ref=lum.at[:, pl.ds(target, HALO), :],
-            send_sem=halo_send.at[side], recv_sem=halo_recv.at[side],
+            src_ref=lum.at[:, pl.ds(source, HALO), lanes],
+            dst_ref=lum.at[:, pl.ds(target, HALO), lanes],
+            send_sem=halo_send.at[side, part], recv_sem=halo_recv.at[side, part],
             device_id={"tile": peer}, device_id_type=pl.DeviceIdType.MESH,
         )
 
@@ -168,7 +172,8 @@
 
     @pl.when(tile > 0)
     def _():
-        halo_copy(0).start()
+        for part in range(pairs):
+            halo_copy(0, part).start()
 
     @pl.when(tile == 0)
     def _():
@@ -179,7 +184,8 @@
 
     @pl.when(tile < tiles - 1)
     def _():
-        halo_copy(1).start()
+        for part in range(pairs):
+            halo_copy(1, part).start()
 
     @pl.when(tile == tiles - 1)
     def _():
@@ -193,8 +199,9 @@
     def columns(pair, spans):
         for k in range(2):
             block = pair * 2 + k
-            variant = jnp.where(block == 0, 0, jnp.where(block == 2 * pairs - 1, 2, 1))
-            window = pl.ds(pl.multiple_of(block * LANES, LANES), 2 * LANES)
+            variant = 0 if block == 0 else 2 if block == 2 * pairs - 1 else 1
+            window = pl.ds(block * LANES, 2 * LANES)
+            smooth = smooths[pair]
             cells = jnp.concatenate(
                 [
                     lum[plane, start : start + count, window]
@@ -214,25 +221,27 @@
                 for start, count in spans:
                     spot = pl.ds(start * 8 + plane * 2 + k, count, stride=8)
                     part = slice(at, at + count)
-                    smooth[pair, 0, spot, :] = low[part, :LANES]
-                    smooth[pair, 1, spot, :] = low[part, LANES:]
-                    smooth[pair, 2, spot, :] = high[part, :LANES]
-                    smooth[pair, 3, spot, :] = high[part, LANES:]
+                    smooth[0, spot, :] = low[part, :LANES]
+                    smooth[1, spot, :] = low[part, LANES:]
+                    smooth[2, spot, :] = high[part, :LANES]
+                    smooth[3, spot, :] = high[part, LANES:]
                     at += count
 
-    def inner_columns(pair, carry):
-        columns(pair, ((HALO, rows),))
-        return carry
-
-    lax.fori_loop(0, pairs, inner_columns, 0)
-
-    @pl.when(tile < tiles - 1)
-    def _():
-        halo_copy(0).wait_recv()
-
-    @pl.when(tile > 0)
-    def _():
-        halo_copy(1).wait_recv()
+    inner = ((HALO, rows),)
+    outer = ((0, HALO), (HALO + rows, HALO))
+    for pair in range(AHEAD):
+        columns(pair, inner)
+
+    def outer_columns(pair):
+        @pl.when(tile < tiles - 1)
+        def _():
+            halo_copy(0, pair).wait_recv()
+
+        @pl.when(tile > 0)
+        def _():
+            halo_copy(1, pair).wait_recv()
+
+        columns(pair, outer)
 
     keep = (jnp.where(tile == 0, 0.0, 1.0), jnp.where(tile == tiles - 1, 0.0, 1.0))
 
@@ -240,7 +249,7 @@
         for level in range(LEVELS, 0, -1):
             chain = CHAINS[level]
             reach = sum(2 * stride for stride, _ in chain)
-            own = smooth.at[pair, level - 1]
+            own = smooths[pair].at[level - 1]
             source = own
             for index, (stride, outputs) in enumerate(chain):
                 reach -= 2 * stride
@@ -257,7 +266,7 @@
             here = pl.ds(pl.multiple_of(block * 64, 64), 64)
             wide = pl.ds(pl.multiple_of(block * 64 + HALO * 8, 64), 64)
             approx = [field[pair, here, :], buf_a[wide, :]]
-            approx += [smooth[pair, level, wide, :] for level in range(1, LEVELS)]
+            approx += [smooths[pair][level, wide, :] for level in range(1, LEVELS)]
             energy = None
             for level in range(LEVELS):
                 detail = approx[level] - approx[level + 1]
@@ -333,8 +342,11 @@
                 for channel in range(3):
                     means_two[pair, half, second, channel] = colours[channel].astype(jnp.bfloat16)
 
-    def one_pair(pair, carry):
-        columns(pair, ((0, HALO), (HALO + rows, HALO)))
+    def one_pair(pair):
+        if pair + AHEAD < pairs:
+            columns(pair + AHEAD, inner)
+        if pair + 1 < pairs:
+            outer_columns(pair + 1)
         rows_smoothed(pair)
         scored(pair)
         states(pair)
@@ -343,11 +355,8 @@
                 for copy in first_copies(pair, half, step):
                     copy.start()
 
-        @pl.when(pair > 1)
-        def _():
+        if pair > 1:
             advance(pair - 2)
-
-        return carry
 
     def advance(pair):
         first_merge(pair)
@@ -382,7 +391,9 @@
             for channel in range(3):
                 out_ref[channel, :, lanes] = colours[channel].astype(jnp.bfloat16)
 
-    lax.fori_loop(0, pairs, one_pair, 0)
+    outer_columns(0)
+    for pair in range(pairs):
+        one_pair(pair)
     advance(pairs - 2)
     advance(pairs - 1)
     for pair in range(pairs):
@@ -390,11 +401,13 @@
 
     @pl.when(tile > 0)
     def _():
-        halo_copy(0).wait_send()
+        for part in range(pairs):
+            halo_copy(0, part).wait_send()
 
     @pl.when(tile < tiles - 1)
     def _():
-        halo_copy(1).wait_send()
+        for part in range(pairs):
+            halo_copy(1, part).wait_send()
 
     def drain(pair, carry):
         for half in range(2):
@@ -427,7 +440,10 @@
             pltpu.VMEM(weights.shape, jnp.bfloat16),
             pltpu.VMEM((SIDE, extent, width + LANES), jnp.bfloat16),
             pltpu.VMEM((pairs, rows * 8, LANES), jnp.float32),
-            pltpu.VMEM((pairs, LEVELS, extent * 8, LANES), jnp.float32),
+            pltpu.VMEM((LEVELS, extent * 8, LANES), jnp.float32),
+            pltpu.VMEM((LEVELS, extent * 8, LANES), jnp.float32),
+            pltpu.VMEM((LEVELS, extent * 8, LANES), jnp.float32),
+            pltpu.VMEM((LEVELS, extent * 8, LANES), jnp.float32),
             pltpu.VMEM((extent * 8, LANES), jnp.float32),
             pltpu.VMEM((extent * 8, LANES), jnp.float32),
             pltpu.VMEM((rows * 8, LANES), jnp.float32),
@@ -440,8 +456,8 @@
             pltpu.VMEM((pairs, 2, others, share, LANES), jnp.float32),
             pltpu.VMEM((pairs, 2, others, channels, share, LANES), jnp.bfloat16),
             pltpu.SemaphoreType.DMA((SIDE + 1,)),
-            pltpu.SemaphoreType.DMA((2,)),
-            pltpu.SemaphoreType.DMA((2,)),
+            pltpu.SemaphoreType.DMA((2, pairs)),
+            pltpu.SemaphoreType.DMA((2, pairs)),
             pltpu.SemaphoreType.DMA((2 * pairs, 2, others, 2)),
             pltpu.SemaphoreType.DMA((2 * pairs, 2, others, 2)),
         ],

time: 32.3 us -> 31.3 us (0.969); the launches traced: 31.7 us -> 31.1 us
  Pallas kernels: 30.2 us -> 29.7 us
    pallas_call x1, Pallas kernels: 30.2 us -> 29.7 us  [per_device(): pl.pallas_call(focus_kernel, out_shape=jax.ShapeDtypeStruct((channels, sh...]
where the time goes in v4:
time: 31.3 us; the launch traced here: 31.1 us
  Pallas kernels  29.7 us (95%)
  local copies, waits for them, and re-layouts  1.42 us (5%)
    pallas_call x1, Pallas kernels, per_device(): pl.pallas_call(focus_kernel, out_shape=jax.ShapeDtypeStruct((channels, sh...  29.7 us
    unnamed x1, local copies, waits for them, and re-layouts  1.42 us

profile of v4, /device:TPU:1, one launch (start us, length us, event | category | flops | bytes accessed | tf_op | source)
XLA Modules:
  0.0 31.1 jit_solution(8608620263019298639)
XLA Ops:
  0.0 29.7 %shard_map.37 = bf16[3,8,1024]{2,1,0:T(8,128)(2,1)} custom-call(f32[4]{0:T(128)} %gain_ref.1, bf16[4,3,128,1024]{3,2,1,0:T(8,128)(2,1)} %planes_hbm.1, bf16[3,256,768]{2,1,0:T(8,128)(2,1)} %constant.2.clone.weights_hbm), custom_call_target="tpu_custom_call" | custom-call | tf_op jit(solution)/shard_map/pallas_call | solution.py:429
  29.7 1.4 %copy.5 = bf16[3,8,1024]{2,1,0:T(8,128)(2,1)} copy(bf16[3,8,1024]{2,1,0:T(8,128)(2,1)} %shard_map.37) | data formatting | bytes 98304

commit v5 on v4

--- a/solution.py
+++ b/solution.py
@@ -19,10 +19,11 @@
     3: ((1, 19), (2, 18), (4, 16)),
     4: ((1, 23), (2, 22), (4, 20), (8, 16)),
 }
-AHEAD = 3
-UNROLL_LUM = 2
-UNROLL_SCORE = 2
-UNROLL_STATES = 2
+AHEAD = 4
+EXTRA = 1
+UNROLL_LUM = 8
+UNROLL_SCORE = 16
+UNROLL_STATES = 8
 
 
 def column_weights(width):
@@ -277,34 +278,33 @@
 
         lax.fori_loop(0, rows // 8, body, 0, unroll=UNROLL_SCORE)
 
-    def states(pair):
+    def states(pair, k):
         def body(block, carry):
             here = pl.ds(pl.multiple_of(block * 16, 16), 16)
             far = block // 2
             near = (block - far * 2) * 2
-            for k in range(2):
-                lanes = pl.ds(pl.multiple_of((pair * 2 + k) * LANES, LANES), LANES)
-                parts = [
-                    score[pl.ds(block * 128 + plane * 2 + k, 16, stride=8), :] for plane in range(SIDE)
-                ]
-                top = jnp.maximum(jnp.maximum(parts[0], parts[1]), jnp.maximum(parts[2], parts[3]))
-                shares = [jnp.exp(part - top) for part in parts]
-                total = (shares[0] + shares[1]) + (shares[2] + shares[3])
-                inverse = 1.0 / total
-                shares = [share * inverse for share in shares]
-                log_sum = top + jnp.log(total)
-                spots = ((far, near), (far, near + 1)) if k == 0 else ((near, far), (near + 1, far))
+            lanes = pl.ds(pl.multiple_of((pair * 2 + k) * LANES, LANES), LANES)
+            parts = [
+                score[pl.ds(block * 128 + plane * 2 + k, 16, stride=8), :] for plane in range(SIDE)
+            ]
+            top = jnp.maximum(jnp.maximum(parts[0], parts[1]), jnp.maximum(parts[2], parts[3]))
+            shares = [jnp.exp(part - top) for part in parts]
+            total = (shares[0] + shares[1]) + (shares[2] + shares[3])
+            inverse = 1.0 / total
+            shares = [share * inverse for share in shares]
+            log_sum = top + jnp.log(total)
+            spots = ((far, near), (far, near + 1)) if k == 0 else ((near, far), (near + 1, far))
+            for part, (first, second) in enumerate(spots):
+                logs_zero[pair, k, first, second] = log_sum[part * 8 : part * 8 + 8]
+            for channel in range(3):
+                mean = shares[0] * planes[0, channel, here, lanes].astype(jnp.float32)
+                for plane in range(1, SIDE):
+                    mean = mean + shares[plane] * planes[plane, channel, here, lanes].astype(
+                        jnp.float32
+                    )
+                mean = mean.astype(jnp.bfloat16)
                 for part, (first, second) in enumerate(spots):
-                    logs_zero[pair, k, first, second] = log_sum[part * 8 : part * 8 + 8]
-                for channel in range(3):
-                    mean = shares[0] * planes[0, channel, here, lanes].astype(jnp.float32)
-                    for plane in range(1, SIDE):
-                        mean = mean + shares[plane] * planes[plane, channel, here, lanes].astype(
-                            jnp.float32
-                        )
-                    mean = mean.astype(jnp.bfloat16)
-                    for part, (first, second) in enumerate(spots):
-                        means_zero[pair, k, first, second, channel] = mean[part * 8 : part * 8 + 8]
+                    means_zero[pair, k, first, second, channel] = mean[part * 8 : part * 8 + 8]
             return carry
 
         lax.fori_loop(0, rows // 16, body, 0, unroll=UNROLL_STATES)
@@ -323,45 +323,44 @@
             )
         ]
 
-    def first_merge(pair):
+    def first_merge(pair, half):
+        own = row if half == 0 else col
+        for step in STEPS:
+            for copy in first_copies(pair, half, step):
+                copy.wait_recv()
+
+        for second in range(SIDE):
+            logs = [logs_zero[pair, half, own, second]]
+            logs += [logs_one[pair, half, k, second] for k in range(SIDE - 1)]
+            means = [means_zero[pair, half, own, second].astype(jnp.float32)]
+            means += [
+                means_one[pair, half, k, second].astype(jnp.float32) for k in range(SIDE - 1)
+            ]
+            top, total, colours = merged_states(logs, means)
+            logs_two[pair, half, second] = top + jnp.log(total)
+            for channel in range(3):
+                means_two[pair, half, second, channel] = colours[channel].astype(jnp.bfloat16)
+
+    def one_pair(pair):
+        if pair > 0:
+            if AHEAD <= pair + EXTRA < pairs:
+                columns(pair + EXTRA, inner)
+            outer_columns(pair)
+        rows_smoothed(pair)
+        scored(pair)
         for half in range(2):
-            own = row if half == 0 else col
+            states(pair, half)
             for step in STEPS:
                 for copy in first_copies(pair, half, step):
-                    copy.wait_recv()
-
-            for second in range(SIDE):
-                logs = [logs_zero[pair, half, own, second]]
-                logs += [logs_one[pair, half, k, second] for k in range(SIDE - 1)]
-                means = [means_zero[pair, half, own, second].astype(jnp.float32)]
-                means += [
-                    means_one[pair, half, k, second].astype(jnp.float32) for k in range(SIDE - 1)
-                ]
-                top, total, colours = merged_states(logs, means)
-                logs_two[pair, half, second] = top + jnp.log(total)
-                for channel in range(3):
-                    means_two[pair, half, second, channel] = colours[channel].astype(jnp.bfloat16)
-
-    def one_pair(pair):
-        if pair + AHEAD < pairs:
-            columns(pair + AHEAD, inner)
-        if pair + 1 < pairs:
-            outer_columns(pair + 1)
-        rows_smoothed(pair)
-        scored(pair)
-        states(pair)
-        for step in STEPS:
-            for half in range(2):
-                for copy in first_copies(pair, half, step):
                     copy.start()
 
         if pair > 1:
             advance(pair - 2)
 
     def advance(pair):
-        first_merge(pair)
-        for step in STEPS:
-            for half in range(2):
+        for half in range(2):
+            first_merge(pair, half)
+            for step in STEPS:
                 for copy in last_copies(pair, half, step):
                     copy.start()
 

time: 31.3 us -> 30.3 us (0.968)
  Pallas kernels: 29.7 us -> 28.7 us
    pallas_call x1, Pallas kernels: 29.7 us -> 28.7 us  [per_device(): pl.pallas_call(focus_kernel, out_shape=jax.ShapeDtypeStruct((channels, sh...]
where the time goes in v5:
time: 30.3 us; the launch traced here: 30.2 us
  Pallas kernels  28.7 us (95%)
  local copies, waits for them, and re-layouts  1.42 us (5%)
    pallas_call x1, Pallas kernels, per_device(): pl.pallas_call(focus_kernel, out_shape=jax.ShapeDtypeStruct((channels, sh...  28.7 us
    unnamed x1, local copies, waits for them, and re-layouts  1.42 us

profile of v5, /device:TPU:1, one launch (start us, length us, event | category | flops | bytes accessed | tf_op | source)
XLA Modules:
  0.0 30.2 jit_solution(13268833623232171578)
XLA Ops:
  0.0 28.7 %shard_map.37 = bf16[3,8,1024]{2,1,0:T(8,128)(2,1)} custom-call(f32[4]{0:T(128)} %gain_ref.1, bf16[4,3,128,1024]{3,2,1,0:T(8,128)(2,1)} %planes_hbm.1, bf16[3,256,768]{2,1,0:T(8,128)(2,1)} %constant.2.clone.weights_hbm), custom_call_target="tpu_custom_call" | custom-call | tf_op jit(solution)/shard_map/pallas_call | solution.py:428
  28.7 1.4 %copy.5 = bf16[3,8,1024]{2,1,0:T(8,128)(2,1)} copy(bf16[3,8,1024]{2,1,0:T(8,128)(2,1)} %shard_map.37) | data formatting | bytes 98304

commit v6 on v5

--- a/solution.py
+++ b/solution.py
@@ -173,8 +173,7 @@
 
     @pl.when(tile > 0)
     def _():
-        for part in range(pairs):
-            halo_copy(0, part).start()
+        halo_copy(0, 0).start()
 
     @pl.when(tile == 0)
     def _():
@@ -185,12 +184,21 @@
 
     @pl.when(tile < tiles - 1)
     def _():
-        for part in range(pairs):
+        halo_copy(1, 0).start()
+
+    @pl.when(tile == tiles - 1)
+    def _():
+        lum[:, HALO + rows : extent, :] = jnp.zeros((SIDE, HALO, width + LANES), jnp.bfloat16)
+
+    @pl.when(tile > 0)
+    def _():
+        for part in range(1, pairs):
+            halo_copy(0, part).start()
+
+    @pl.when(tile < tiles - 1)
+    def _():
+        for part in range(1, pairs):
             halo_copy(1, part).start()
-
-    @pl.when(tile == tiles - 1)
-    def _():
-        lum[:, HALO + rows : extent, :] = jnp.zeros((SIDE, HALO, width + LANES), jnp.bfloat16)
 
     for q in (1, 2):
         loads[q].wait()
@@ -393,10 +401,23 @@
     outer_columns(0)
     for pair in range(pairs):
         one_pair(pair)
+    def drain_first(pair):
+        for half in range(2):
+            for step in STEPS:
+                for copy in first_copies(pair, half, step):
+                    copy.wait_send()
+
+    def drain_last(pair):
+        for half in range(2):
+            for step in STEPS:
+                for copy in last_copies(pair, half, step):
+                    copy.wait_send()
+
     advance(pairs - 2)
+    for pair in range(pairs - 1):
+        drain_first(pair)
+    last_merge(0)
     advance(pairs - 1)
-    for pair in range(pairs):
-        last_merge(pair)
 
     @pl.when(tile > 0)
     def _():
@@ -408,14 +429,12 @@
         for part in range(pairs):
             halo_copy(1, part).wait_send()
 
-    def drain(pair, carry):
-        for half in range(2):
-            for step in STEPS:
-                for copy in first_copies(pair, half, step) + last_copies(pair, half, step):
-                    copy.wait_send()
-        return carry
-
-    lax.fori_loop(0, pairs, drain, 0)
+    drain_first(pairs - 1)
+    for pair in range(pairs - 1):
+        drain_last(pair)
+    for pair in range(1, pairs):
+        last_merge(pair)
+    drain_last(pairs - 1)
 
 
 def per_device(planes, level_gain):

time: 30.3 us -> 30.2 us (level)
  no operation moved by 1% of the time
where the time goes in v6:
time: 30.2 us; the launch traced here: 30 us
  Pallas kernels  28.6 us (95%)
  local copies, waits for them, and re-layouts  1.42 us (5%)
    pallas_call x1, Pallas kernels, per_device(): pl.pallas_call(focus_kernel, out_shape=jax.ShapeDtypeStruct((channels, sh...  28.6 us
    unnamed x1, local copies, waits for them, and re-layouts  1.42 us

profile of v6, /device:TPU:1, one launch (start us, length us, event | category | flops | bytes accessed | tf_op | source)
XLA Modules:
  0.0 30.0 jit_solution(3928914241863704144)
XLA Ops:
  0.0 28.6 %shard_map.37 = bf16[3,8,1024]{2,1,0:T(8,128)(2,1)} custom-call(f32[4]{0:T(128)} %gain_ref.1, bf16[4,3,128,1024]{3,2,1,0:T(8,128)(2,1)} %planes_hbm.1, bf16[3,256,768]{2,1,0:T(8,128)(2,1)} %constant.2.clone.weights_hbm), custom_call_target="tpu_custom_call" | custom-call | tf_op jit(solution)/shard_map/pallas_call | solution.py:447
  28.6 1.4 %copy.5 = bf16[3,8,1024]{2,1,0:T(8,128)(2,1)} copy(bf16[3,8,1024]{2,1,0:T(8,128)(2,1)} %shard_map.37) | data formatting | bytes 98304
